TPU v7x, 32 devices: a whole 2x2x4 slice. The times are simulated.
32 devices in a mesh: tiles: 8 (over z, y), rhs: 4 (over x, core).
Axes of the slice: x: 2, y: 2, z: 4, core: 2. Of those that a mesh axis runs over, the one named last changes fastest.
Arguments:
- rhs_rows: bfloat16 [256, 8192], P('rhs', 'tiles'), may hold values from -6 to 6
- diag_inverse: bfloat16 [8192, 1024], P('tiles', 'rhs'), may hold values from -0.0625 to 0.5625
- u_factors: bfloat16 [8, 7, 1024, 128], P('tiles'), may hold values from -0.1875 to 0.1875
- v_factors: bfloat16 [8, 7, 1024, 128], P('tiles'), may hold values from -0.1875 to 0.1875
- tile_rows: int32 [8, 7], P('tiles'), may hold values from 0 to 7, as said below
- tile_ranks: int32 [8, 7], P('tiles'), may hold values from 16 to 128
- point_coords: float32 [8, 8192], P(None, 'tiles'), may hold values from 0 to 1
- cand_coords: float32 [8, 128], P(None, 'rhs'), may hold values from 0 to 1
- owner: int32 [128], P('rhs'), may hold values from 0 to 7, as said below
Outputs:
- solution: bfloat16 [256, 8192], P('rhs', 'tiles')
- predictions: float32 [128, 256], P(('tiles', 'rhs'))
Inputs may be any that keep to these rules, and one draw needn't show every extreme that they name: Each tile column lists 7 distinct tile rows, none equal to itself; for each slot k, tile_rows[., k] is a permutation of the tile rows. `owner`: in each group of 32 consecutive candidates every tile owns exactly 4.
All inputs are finite; a program needn't handle non-finite values.
Results may differ from a plain program's by a relative error of at most 0.008.
Values may be sent and summed in bfloat16 or wider, within the bound.
No kernel may reach another device: no remote copies, remote signals or barrier semaphores. Data moves between devices by JAX's collectives and lax.ppermute only.
A program may use at most 64 MiB of HBM per device.

v0:
```python
import math
import jax
import jax.numpy as jnp
from jax import lax
from jax.sharding import PartitionSpec as P

ITERS = 2


def kernel_block(cand, cand_sq, points, amplitude):
    point_sq = jnp.sum(points * points, 0)
    inner_products = lax.dot_general(
        cand, points, (((0,), (0,)), ((), ())), precision=lax.Precision.HIGHEST
    )
    dist_sq = cand_sq[:, None] + point_sq[None, :] - 2.0 * inner_products
    return (jnp.exp(-2.0 * dist_sq) * amplitude).astype(jnp.bfloat16)


def per_device(
    rhs_rows,
    diag_inverse,
    u_factors,
    v_factors,
    tile_rows,
    tile_ranks,
    point_coords,
    cand_coords,
    owner,
):
    tiles_count = lax.axis_size("tiles")
    tile_here = lax.axis_index("tiles")
    u_slots = u_factors[0]
    v_slots = v_factors[0]
    width = u_slots.shape[2]
    slot_count = u_slots.shape[0]
    rank_mask = (
        lax.broadcasted_iota(jnp.int32, (slot_count, width), 1) < tile_ranks[0][:, None]
    ).astype(jnp.bfloat16)
    peer_ids = jnp.arange(tiles_count, dtype=jnp.int32)
    all_rows = lax.all_gather(tile_rows, "tiles", axis=0, tiled=True)
    slot_range = jnp.arange(slot_count, dtype=jnp.int32)
    column_ids = jnp.broadcast_to(peer_ids[:, None], all_rows.shape)
    all_sources = (
        jnp.zeros(all_rows.shape, jnp.int32).at[all_rows, slot_range[None, :]].set(column_ids)
    )
    sources_here = lax.dynamic_slice_in_dim(all_sources, tile_here, 1, 0)[0]
    to_rows = (peer_ids[:, None] == tile_rows[0][None, :]).astype(jnp.bfloat16)
    to_cols = (peer_ids[:, None] == sources_here[None, :]).astype(jnp.bfloat16)
    whole_inverse = lax.all_gather(diag_inverse, "rhs", axis=1, tiled=True)

    def precondition(resid):
        return jnp.dot(resid, whole_inverse, preferred_element_type=jnp.float32).astype(
            jnp.bfloat16
        )

    iterate = precondition(rhs_rows)
    for sweep in range(ITERS):
        lower = jnp.einsum("cb,kbr->kcr", iterate, v_slots, preferred_element_type=jnp.float32)
        lower = (lower * rank_mask[:, None, :]).astype(jnp.bfloat16)
        upper = jnp.einsum(
            "cb,kbr->kcr", iterate, u_slots, preferred_element_type=jnp.float32
        ).astype(jnp.bfloat16)
        send_lower = jnp.einsum(
            "nk,kcr->ncr", to_rows, lower, preferred_element_type=jnp.float32
        ).astype(jnp.bfloat16)
        send_upper = jnp.einsum(
            "nk,kcr->ncr", to_cols, upper, preferred_element_type=jnp.float32
        ).astype(jnp.bfloat16)
        from_picked = jnp.einsum(
            "nk,ncr->kcr",
            to_cols,
            lax.all_to_all(send_lower, "tiles", split_axis=0, concat_axis=0, tiled=True),
            preferred_element_type=jnp.float32,
        ).astype(jnp.bfloat16)
        first = jnp.einsum("kcr,kbr->cb", from_picked, u_slots, preferred_element_type=jnp.float32)
        picked = jnp.einsum(
            "nk,ncr->kcr",
            to_rows,
            lax.all_to_all(send_upper, "tiles", split_axis=0, concat_axis=0, tiled=True),
            preferred_element_type=jnp.float32,
        ).astype(jnp.bfloat16)
        picked = picked * rank_mask[:, None, :]
        second = jnp.einsum("kcr,kbr->cb", picked, v_slots, preferred_element_type=jnp.float32)
        resid = (rhs_rows.astype(jnp.float32) - (first + second)).astype(jnp.bfloat16)
        iterate = precondition(resid)
    block_len = u_slots.shape[1]
    amplitude = 4.0 / math.sqrt(block_len * tiles_count)
    cand_sq = jnp.sum(cand_coords * cand_coords, 0)
    cross = kernel_block(cand_coords, cand_sq, point_coords, amplitude)
    partial_values = lax.dot_general(
        cross,
        lax.all_gather(iterate, "rhs", axis=0, tiled=True),
        (((1,), (1,)), ((), ())),
        preferred_element_type=jnp.float32,
    )
    group_len = owner.shape[0]
    owned = group_len // tiles_count
    owner_hot = (owner[:, None] == peer_ids[None, :]).astype(jnp.int32)
    running = jnp.cumsum(owner_hot, axis=0)
    slot_of = owner * owned + jnp.sum(running * owner_hot, axis=1) - 1
    ordered = jnp.zeros_like(partial_values).at[slot_of].set(partial_values)
    summed = lax.psum(ordered, "tiles")
    owned_sums = lax.dynamic_slice_in_dim(summed, tile_here * owned, owned, 0)
    return (iterate, owned_sums)


def solution(mesh):
    in_specs = (
        P("rhs", "tiles"),
        P("tiles", "rhs"),
        P("tiles", None, None, None),
        P("tiles", None, None, None),
        P("tiles", None),
        P("tiles", None),
        P(None, "tiles"),
        P(None, "rhs"),
        P("rhs"),
    )
    out_specs = (P("rhs", "tiles"), P(("tiles", "rhs"), None))
    return jax.shard_map(
        per_device, mesh=mesh, in_specs=in_specs, out_specs=out_specs, check_vma=False
    )
```

profile of v0, /device:TPU:0, one launch (start us, length us, event | category | flops | bytes accessed | tf_op | source)
XLA Modules:
  0.0 142.5 jit_solution(6352598870871334731)
XLA Ops:
  7.2 0.7 all-gather.3.cloned.1.call-update
  7.9 22.5 %all-gather = s32[8,1,7]{2,1,0:T(1,128)S(1)} all-gather(s32[1,1,7]{2,1,0:T(1,128)} %bitcast.143), channel_id=1, replica_groups=mesh['tiles'=8,'rhs'=4] {'tiles'}, dimensions={0}, use_global_device_ids=true | all-gather | bytes 252 | tf_op jit(solution)/shard_map/all_gather | solution.py:40
  30.6 0.7 fusion.107
  31.4 3.5 %scatter_fusion = s32[8,7]{1,0:T(8,128)S(1)} fusion(s32[8,7]{1,0:T(8,128)S(1)} %broadcast.30, s32[56]{0:T(128)S(1)} %reshape.46, s32[56]{0:T(128)S(1)} %reshape.48), kind=kCustom, calls=%fused_computation | custom fusion | bytes 1120 | tf_op jit(solution)/shard_map/scatter | solution.py:44
  35.2 0.3 fusion.90
  35.6 2.2 %fusion.71 = bf16[64,1024,1]{1,0,2:T(8,128)(2,1)S(1)} fusion(bf16[64,1024]{1,0:T(8,128)(2,1)S(1)} %copy-done.2, bf16[1024,1024]{1,0:T(8,128)(2,1)} %all-gather.3.cloned.1.call-done), kind=kOutput, calls=%fused_computation.46 | convolution fusion | flops 134283264 | bytes 2359296 | tf_op jit(solution)/shard_map/dot_general | solution.py:52
  37.9 0.4 fusion.87
  38.5 0.7 copy.30
  39.2 5.0 %all-to-all-start.1 = ((bf16[8,64,128]{2,1,0:T(8,128)(2,1)}), bf16[8,64,128]{2,1,0:T(8,128)(2,1)S(1)}, u32[]{:S(2)}, u32[]{:S(2)}) async-start(bf16[8,64,128]{2,1,0:T(8,128)(2,1)} %copy.30), calls=%async_computation.1 | async-start | bytes 262144 | tf_op jit(solution)/shard_map/all_to_all | solution.py:79
  44.2 0.4 fusion.78
  44.6 0.3 convolution_convert_fusion.10
  44.9 0.7 copy.25
  45.6 6.0 %all-to-all-done.1 = bf16[8,64,128]{2,1,0:T(8,128)(2,1)S(1)} async-done(((bf16[8,64,128]{2,1,0:T(8,128)(2,1)}), bf16[8,64,128]{2,1,0:T(8,128)(2,1)S(1)}, u32[]{:S(2)}, u32[]{:S(2)}) %all-to-all-start.1) | async-done | bytes 131104 | tf_op jit(solution)/shard_map/all_to_all | solution.py:79
  51.6 3.4 %all-to-all-start = ((bf16[8,64,128]{2,1,0:T(8,128)(2,1)}), bf16[8,64,128]{2,1,0:T(8,128)(2,1)S(1)}, u32[]{:S(2)}, u32[]{:S(2)}) async-start(bf16[8,64,128]{2,1,0:T(8,128)(2,1)} %copy.25), calls=%async_computation | async-start | bytes 262144 | tf_op jit(solution)/shard_map/all_to_all | solution.py:72
  55.2 0.7 fusion.16
  55.9 6.4 %all-to-all-done = bf16[8,64,128]{2,1,0:T(8,128)(2,1)S(1)} async-done(((bf16[8,64,128]{2,1,0:T(8,128)(2,1)}), bf16[8,64,128]{2,1,0:T(8,128)(2,1)S(1)}, u32[]{:S(2)}, u32[]{:S(2)}) %all-to-all-start) | async-done | bytes 131104 | tf_op jit(solution)/shard_map/all_to_all | solution.py:72
  62.5 3.2 %fusion.68 = bf16[64,1024,1]{1,0,2:T(8,128)(2,1)S(1)} fusion(bf16[1024,1024]{1,0:T(8,128)(2,1)} %all-gather.3.cloned.1.call-done, f32[64,1024]{1,0:T(8,128)S(1)} %fusion.16, bf16[1,7,1024,128]{3,2,1,0:T(8,128)(2,1)} %param.11, bf16[64,1024]{1,0:T(8,128)(2,1)S(1)} %copy-done.2, bf16[7,64,128]{2,0,1:T(8,128)(2,1)S(1)} %convolution_convert_fusion.9), kind=kOutput, calls=%fused_computation.45 | convolution fusion | flops 251985920 | bytes 4571136 | tf_op jit(solution)/shard_map/dot_general | solution.py:52
  65.7 1.9 %fusion.84 = bf16[7,64,128]{2,1,0:T(8,128)(2,1)S(1)} fusion(bf16[64,1024,1]{1,0,2:T(8,128)(2,1)S(1)} %fusion.68, bf16[1,7,1024,128]{3,2,1,0:T(8,128)(2,1)} %param.11), kind=kOutput, calls=%fused_computation.56 | convolution fusion | flops 117497856 | bytes 2080768 | tf_op jit(solution)/shard_map/cb,kbr->kcr/dot_general | solution.py:60
  67.6 0.4 fusion.81
  68.2 0.7 copy.40
  68.9 3.4 %all-to-all-start.3 = ((bf16[8,64,128]{2,1,0:T(8,128)(2,1)}), bf16[8,64,128]{2,1,0:T(8,128)(2,1)S(1)}, u32[]{:S(2)}, u32[]{:S(2)}) async-start(bf16[8,64,128]{2,1,0:T(8,128)(2,1)} %copy.40), calls=%async_computation.3 | async-start | bytes 262144 | tf_op jit(solution)/shard_map/all_to_all | solution.py:79
  72.3 0.3 convolution_convert_fusion.6
  72.6 0.7 copy.35
  73.3 6.3 %all-to-all-done.3 = bf16[8,64,128]{2,1,0:T(8,128)(2,1)S(1)} async-done(((bf16[8,64,128]{2,1,0:T(8,128)(2,1)}), bf16[8,64,128]{2,1,0:T(8,128)(2,1)S(1)}, u32[]{:S(2)}, u32[]{:S(2)}) %all-to-all-start.3) | async-done | bytes 131104 | tf_op jit(solution)/shard_map/all_to_all | solution.py:79
  79.6 3.4 %all-to-all-start.2 = ((bf16[8,64,128]{2,1,0:T(8,128)(2,1)}), bf16[8,64,128]{2,1,0:T(8,128)(2,1)S(1)}, u32[]{:S(2)}, u32[]{:S(2)}) async-start(bf16[8,64,128]{2,1,0:T(8,128)(2,1)} %copy.35), calls=%async_computation.2 | async-start | bytes 262144 | tf_op jit(solution)/shard_map/all_to_all | solution.py:72
  83.2 0.7 fusion.19
  83.9 6.4 %all-to-all-done.2 = bf16[8,64,128]{2,1,0:T(8,128)(2,1)S(1)} async-done(((bf16[8,64,128]{2,1,0:T(8,128)(2,1)}), bf16[8,64,128]{2,1,0:T(8,128)(2,1)S(1)}, u32[]{:S(2)}, u32[]{:S(2)}) %all-to-all-start.2) | async-done | bytes 131104 | tf_op jit(solution)/shard_map/all_to_all | solution.py:72
  90.5 3.2 %convolution_convert_fusion = bf16[64,1024]{1,0:T(8,128)(2,1)S(1)} fusion(bf16[1024,1024]{1,0:T(8,128)(2,1)} %all-gather.3.cloned.1.call-done, f32[64,1024]{1,0:T(8,128)S(1)} %fusion.19, bf16[1,7,1024,128]{3,2,1,0:T(8,128)(2,1)} %param.11, bf16[64,1024]{1,0:T(8,128)(2,1)S(1)} %copy-done.2, bf16[7,64,128]{2,0,1:T(8,128)(2,1)S(1)} %convolution_convert_fusion.5), kind=kOutput, calls=%fused_computation.30 | convolution fusion | flops 251985920 | bytes 4571136 | tf_op jit(solution)/shard_map/dot_general | solution.py:52
  93.7 6.5 %all_gather.11 = bf16[256,1024]{1,0:T(8,128)(2,1)S(1)} all-gather(bf16[64,1024]{1,0:T(8,128)(2,1)S(1)} %convolution_convert_fusion), channel_id=1, replica_groups=mesh['tiles'=8,'rhs'=4] {'rhs'}, dimensions={0}, use_global_device_ids=true | all-gather | bytes 655360 | tf_op jit(solution)/shard_map/all_gather | solution.py:92
  100.4 0.7 scatter_custom_fusion.1
  101.2 33.9 %psum.7 = f32[32,256]{1,0:T(8,128)S(1)} all-reduce(f32[32,256]{1,0:T(8,128)S(1)} %scatter_custom_fusion.1), channel_id=1, replica_groups=mesh['tiles'=8,'rhs'=4] {'tiles'}, use_global_device_ids=true, to_apply=%region_6.7 | all-reduce | flops 8192 | bytes 65536 | tf_op jit(solution)/shard_map/psum | solution.py:102
  135.1 0.6 constant_dynamic-slice_fusion
  (39 shorter events, 2.2 us)
Async XLA Ops:
  7.2 37.0 %copy-start = (bf16[1,7,1024,128]{3,2,1,0:T(8,128)(2,1)S(1)}, bf16[1,7,1024,128]{3,2,1,0:T(8,128)(2,1)}, u32[]{:S(2)}) copy-start(bf16[1,7,1024,128]{3,2,1,0:T(8,128)(2,1)} %param.12) | copy-start | bytes 5505028
  7.2 28.4 %all-gather.3.cloned.1.call-start = ((), (), s32[]{:S(2)}) async-start(), calls=%async_computation.4 | async-start | bytes 2621440 | tf_op jit(solution)/shard_map/all_gather | solution.py:49
  31.4 3.5 %copy-start.6 = (f32[8,32]{1,0:T(8,128)S(1)}, f32[8,32]{1,0:T(8,128)}, u32[]{:S(2)}) copy-start(f32[8,32]{1,0:T(8,128)} %param.16) | copy-start | bytes 3076
  31.4 3.6 %copy-start.4 = (f32[8,1024]{1,0:T(8,128)S(1)}, f32[8,1024]{1,0:T(8,128)}, u32[]{:S(2)}) copy-start(f32[8,1024]{1,0:T(8,128)} %param.15) | copy-start | bytes 98308
  31.4 3.6 %copy-start.7 = (s32[32]{0:T(128)S(1)}, s32[32]{0:T(128)}, u32[]{:S(2)}) copy-start(s32[32]{0:T(128)} %param.17) | copy-start | bytes 388
  31.4 3.8 %copy-start.8 = (s32[1,7]{1,0:T(1,128)S(1)}, s32[1,7]{1,0:T(1,128)}, u32[]{:S(2)}) copy-start(s32[1,7]{1,0:T(1,128)} %param.14) | copy-start | bytes 88
  31.4 4.2 %copy-start.2 = (bf16[64,1024]{1,0:T(8,128)(2,1)S(1)}, bf16[64,1024]{1,0:T(8,128)(2,1)}, u32[]{:S(2)}) copy-start(bf16[64,1024]{1,0:T(8,128)(2,1)} %param.9) | copy-start | bytes 393220
  35.6 2.2 %copy-start.1 = (bf16[1,7,1024,128]{3,2,1,0:T(8,128)(2,1)S(1)}, bf16[1,7,1024,128]{3,2,1,0:T(8,128)(2,1)}, u32[]{:S(2)}) copy-start(bf16[1,7,1024,128]{3,2,1,0:T(8,128)(2,1)} %param.11) | copy-start | bytes 5505028
  38.3 6.3 %copy-start.5 = (s32[1,7]{1,0:T(1,128)S(1)}, s32[1,7]{1,0:T(1,128)}, u32[]{:S(2)}) copy-start(s32[1,7]{1,0:T(1,128)} %param.13) | copy-start | bytes 88
  39.2 12.4 %all-to-all-start.1 = ((bf16[8,64,128]{2,1,0:T(8,128)(2,1)}), bf16[8,64,128]{2,1,0:T(8,128)(2,1)S(1)}, u32[]{:S(2)}, u32[]{:S(2)}) async-start(bf16[8,64,128]{2,1,0:T(8,128)(2,1)} %copy.30), calls=%async_computation.1 | async-start | bytes 262144 | tf_op jit(solution)/shard_map/all_to_all | solution.py:79
  51.6 10.7 %all-to-all-start = ((bf16[8,64,128]{2,1,0:T(8,128)(2,1)}), bf16[8,64,128]{2,1,0:T(8,128)(2,1)S(1)}, u32[]{:S(2)}, u32[]{:S(2)}) async-start(bf16[8,64,128]{2,1,0:T(8,128)(2,1)} %copy.25), calls=%async_computation | async-start | bytes 262144 | tf_op jit(solution)/shard_map/all_to_all | solution.py:72
  68.9 10.7 %all-to-all-start.3 = ((bf16[8,64,128]{2,1,0:T(8,128)(2,1)}), bf16[8,64,128]{2,1,0:T(8,128)(2,1)S(1)}, u32[]{:S(2)}, u32[]{:S(2)}) async-start(bf16[8,64,128]{2,1,0:T(8,128)(2,1)} %copy.40), calls=%async_computation.3 | async-start | bytes 262144 | tf_op jit(solution)/shard_map/all_to_all | solution.py:79
  79.6 10.7 %all-to-all-start.2 = ((bf16[8,64,128]{2,1,0:T(8,128)(2,1)}), bf16[8,64,128]{2,1,0:T(8,128)(2,1)S(1)}, u32[]{:S(2)}, u32[]{:S(2)}) async-start(bf16[8,64,128]{2,1,0:T(8,128)(2,1)} %copy.35), calls=%async_computation.2 | async-start | bytes 262144 | tf_op jit(solution)/shard_map/all_to_all | solution.py:72
  93.7 42.0 %copy-start.3 = (bf16[64,1024]{1,0:T(8,128)(2,1)}, bf16[64,1024]{1,0:T(8,128)(2,1)S(1)}, u32[]{:S(2)}) copy-start(bf16[64,1024]{1,0:T(8,128)(2,1)S(1)} %convolution_convert_fusion) | copy-start | bytes 393220
Sparse Core Ops, SparseCore 0:
  9.5 25.5 all-gather.2
where the time goes:
time: 143 us
  blocking collectives  62.9 us (44%)
  waiting for transfers between devices  25.7 us (18%)
  matrix products  15.6 us (11%)
  starting transfers between devices  15.1 us (11%)
  between operations  14.4 us (10%)
  local copies, waits for them, and re-layouts  7.77 us (5%)
    psum x1, blocking collectives, per_device(): summed = lax.psum(ordered, 'tiles')  33.9 us
    all_gather x1, blocking collectives, per_device(): all_rows = lax.all_gather(tile_rows, 'tiles', axis=0, tiled=True)  22.5 us
    all_to_all x2, waiting for transfers between devices, per_device(): lax.all_to_all(send_lower, 'tiles', split_axis=0, concat_axis=0, tiled=True)  12.7 us
    all_to_all x2, waiting for transfers between devices, per_device(): lax.all_to_all(send_upper, 'tiles', split_axis=0, concat_axis=0, tiled=True)  12.2 us
    dot_general x3, matrix products, precondition(): jnp.dot(resid, whole_inverse, preferred_element_type=jnp.float32)  8.6 us
    all_to_all x2, starting transfers between devices, per_device(): lax.all_to_all(send_upper, 'tiles', split_axis=0, concat_axis=0, tiled=True)  8.37 us
    all_to_all x2, starting transfers between devices, per_device(): lax.all_to_all(send_lower, 'tiles', split_axis=0, concat_axis=0, tiled=True)  6.74 us
    all_gather x1, blocking collectives, per_device(): lax.all_gather(iterate, 'rhs', axis=0, tiled=True)  6.5 us
  transfers between devices with their start and end apart: 5, of which 4 were waited for; matrix products, arithmetic and copies ran while one was open for 6% of the time, Pallas kernels for 0%

commit v1 on v0

--- a/solution.py
+++ b/solution.py
@@ -99,7 +99,8 @@
     running = jnp.cumsum(owner_hot, axis=0)
     slot_of = owner * owned + jnp.sum(running * owner_hot, axis=1) - 1
     ordered = jnp.zeros_like(partial_values).at[slot_of].set(partial_values)
-    summed = lax.psum(ordered, "tiles")
+    parts = lax.all_gather(ordered, "tiles", axis=0, tiled=False)
+    summed = parts.sum(axis=0)
     owned_sums = lax.dynamic_slice_in_dim(summed, tile_here * owned, owned, 0)
     return (iterate, owned_sums)
 

time: 143 us -> 140 us (0.979)
  blocking collectives: 62.9 us -> 59.8 us
    psum x1 -> x0, blocking collectives: 33.9 us -> none  [per_device(): summed = lax.psum(ordered, 'tiles')]
    all_gather x0 -> x1, blocking collectives: none -> 30.9 us  [per_device(): parts = lax.all_gather(ordered, 'tiles', axis=0, tiled=False)]
  transfers between devices with their start and end apart: 5 -> 5, of which waited for: 4 -> 4; matrix products, arithmetic and copies ran while one was open for 6% -> 7% of each run, Pallas kernels for 0% -> 0%
where the time goes in v1:
time: 140 us
  blocking collectives  59.8 us (43%)
  waiting for transfers between devices  25.7 us (18%)
  matrix products  15.6 us (11%)
  starting transfers between devices  15.1 us (11%)
  between operations  14.4 us (10%)
  local copies, waits for them, and re-layouts  7.77 us (6%)
    all_gather x1, blocking collectives, per_device(): parts = lax.all_gather(ordered, 'tiles', axis=0, tiled=False)  30.9 us
    all_gather x1, blocking collectives, per_device(): all_rows = lax.all_gather(tile_rows, 'tiles', axis=0, tiled=True)  22.5 us
    all_to_all x2, waiting for transfers between devices, per_device(): lax.all_to_all(send_lower, 'tiles', split_axis=0, concat_axis=0, tiled=True)  12.7 us
    all_to_all x2, waiting for transfers between devices, per_device(): lax.all_to_all(send_upper, 'tiles', split_axis=0, concat_axis=0, tiled=True)  12.2 us
    dot_general x3, matrix products, precondition(): jnp.dot(resid, whole_inverse, preferred_element_type=jnp.float32)  8.6 us
    all_to_all x2, starting transfers between devices, per_device(): lax.all_to_all(send_upper, 'tiles', split_axis=0, concat_axis=0, tiled=True)  8.37 us
    all_to_all x2, starting transfers between devices, per_device(): lax.all_to_all(send_lower, 'tiles', split_axis=0, concat_axis=0, tiled=True)  6.74 us
    all_gather x1, blocking collectives, per_device(): lax.all_gather(iterate, 'rhs', axis=0, tiled=True)  6.5 us
  transfers between devices with their start and end apart: 5, of which 4 were waited for; matrix products, arithmetic and copies ran while one was open for 7% of the time, Pallas kernels for 0%

profile of v1, /device:TPU:0, one launch (start us, length us, event | category | flops | bytes accessed | tf_op | source)
XLA Modules:
  0.0 139.5 jit_solution(9370438221219623401)
XLA Ops:
  7.2 0.7 all-gather.4.cloned.1.call-update
  7.9 22.5 %all-gather.1 = s32[8,1,7]{2,1,0:T(1,128)S(1)} all-gather(s32[1,1,7]{2,1,0:T(1,128)} %bitcast.145), channel_id=1, replica_groups=mesh['tiles'=8,'rhs'=4] {'tiles'}, dimensions={0}, use_global_device_ids=true | all-gather | bytes 252 | tf_op jit(solution)/shard_map/all_gather | solution.py:40
  30.6 0.7 fusion.107
  31.4 3.5 %scatter_fusion = s32[8,7]{1,0:T(8,128)S(1)} fusion(s32[8,7]{1,0:T(8,128)S(1)} %broadcast.30, s32[56]{0:T(128)S(1)} %reshape.46, s32[56]{0:T(128)S(1)} %reshape.48), kind=kCustom, calls=%fused_computation | custom fusion | bytes 1120 | tf_op jit(solution)/shard_map/scatter | solution.py:44
  35.2 0.3 fusion.90
  35.6 2.2 %fusion.71 = bf16[64,1024,1]{1,0,2:T(8,128)(2,1)S(1)} fusion(bf16[64,1024]{1,0:T(8,128)(2,1)S(1)} %copy-done.2, bf16[1024,1024]{1,0:T(8,128)(2,1)} %all-gather.4.cloned.1.call-done), kind=kOutput, calls=%fused_computation.46 | convolution fusion | flops 134283264 | bytes 2359296 | tf_op jit(solution)/shard_map/dot_general | solution.py:52
  37.9 0.4 fusion.87
  38.5 0.7 copy.50
  39.2 5.0 %all-to-all-start.1 = ((bf16[8,64,128]{2,1,0:T(8,128)(2,1)}), bf16[8,64,128]{2,1,0:T(8,128)(2,1)S(1)}, u32[]{:S(2)}, u32[]{:S(2)}) async-start(bf16[8,64,128]{2,1,0:T(8,128)(2,1)} %copy.50), calls=%async_computation.1 | async-start | bytes 262144 | tf_op jit(solution)/shard_map/all_to_all | solution.py:79
  44.2 0.4 fusion.78
  44.6 0.3 convolution_convert_fusion.10
  44.9 0.7 copy.45
  45.6 6.0 %all-to-all-done.1 = bf16[8,64,128]{2,1,0:T(8,128)(2,1)S(1)} async-done(((bf16[8,64,128]{2,1,0:T(8,128)(2,1)}), bf16[8,64,128]{2,1,0:T(8,128)(2,1)S(1)}, u32[]{:S(2)}, u32[]{:S(2)}) %all-to-all-start.1) | async-done | bytes 131104 | tf_op jit(solution)/shard_map/all_to_all | solution.py:79
  51.6 3.4 %all-to-all-start = ((bf16[8,64,128]{2,1,0:T(8,128)(2,1)}), bf16[8,64,128]{2,1,0:T(8,128)(2,1)S(1)}, u32[]{:S(2)}, u32[]{:S(2)}) async-start(bf16[8,64,128]{2,1,0:T(8,128)(2,1)} %copy.45), calls=%async_computation | async-start | bytes 262144 | tf_op jit(solution)/shard_map/all_to_all | solution.py:72
  55.2 0.7 fusion.16
  55.9 6.4 %all-to-all-done = bf16[8,64,128]{2,1,0:T(8,128)(2,1)S(1)} async-done(((bf16[8,64,128]{2,1,0:T(8,128)(2,1)}), bf16[8,64,128]{2,1,0:T(8,128)(2,1)S(1)}, u32[]{:S(2)}, u32[]{:S(2)}) %all-to-all-start) | async-done | bytes 131104 | tf_op jit(solution)/shard_map/all_to_all | solution.py:72
  62.5 3.2 %fusion.68 = bf16[64,1024,1]{1,0,2:T(8,128)(2,1)S(1)} fusion(bf16[1024,1024]{1,0:T(8,128)(2,1)} %all-gather.4.cloned.1.call-done, f32[64,1024]{1,0:T(8,128)S(1)} %fusion.16, bf16[1,7,1024,128]{3,2,1,0:T(8,128)(2,1)} %param.11, bf16[64,1024]{1,0:T(8,128)(2,1)S(1)} %copy-done.2, bf16[7,64,128]{2,0,1:T(8,128)(2,1)S(1)} %convolution_convert_fusion.9), kind=kOutput, calls=%fused_computation.45 | convolution fusion | flops 251985920 | bytes 4571136 | tf_op jit(solution)/shard_map/dot_general | solution.py:52
  65.7 1.9 %fusion.84 = bf16[7,64,128]{2,1,0:T(8,128)(2,1)S(1)} fusion(bf16[64,1024,1]{1,0,2:T(8,128)(2,1)S(1)} %fusion.68, bf16[1,7,1024,128]{3,2,1,0:T(8,128)(2,1)} %param.11), kind=kOutput, calls=%fused_computation.56 | convolution fusion | flops 117497856 | bytes 2080768 | tf_op jit(solution)/shard_map/cb,kbr->kcr/dot_general | solution.py:60
  67.6 0.4 fusion.81
  68.2 0.7 copy.60
  68.9 3.4 %all-to-all-start.3 = ((bf16[8,64,128]{2,1,0:T(8,128)(2,1)}), bf16[8,64,128]{2,1,0:T(8,128)(2,1)S(1)}, u32[]{:S(2)}, u32[]{:S(2)}) async-start(bf16[8,64,128]{2,1,0:T(8,128)(2,1)} %copy.60), calls=%async_computation.3 | async-start | bytes 262144 | tf_op jit(solution)/shard_map/all_to_all | solution.py:79
  72.3 0.3 convolution_convert_fusion.6
  72.6 0.7 copy.55
  73.3 6.3 %all-to-all-done.3 = bf16[8,64,128]{2,1,0:T(8,128)(2,1)S(1)} async-done(((bf16[8,64,128]{2,1,0:T(8,128)(2,1)}), bf16[8,64,128]{2,1,0:T(8,128)(2,1)S(1)}, u32[]{:S(2)}, u32[]{:S(2)}) %all-to-all-start.3) | async-done | bytes 131104 | tf_op jit(solution)/shard_map/all_to_all | solution.py:79
  79.6 3.4 %all-to-all-start.2 = ((bf16[8,64,128]{2,1,0:T(8,128)(2,1)}), bf16[8,64,128]{2,1,0:T(8,128)(2,1)S(1)}, u32[]{:S(2)}, u32[]{:S(2)}) async-start(bf16[8,64,128]{2,1,0:T(8,128)(2,1)} %copy.55), calls=%async_computation.2 | async-start | bytes 262144 | tf_op jit(solution)/shard_map/all_to_all | solution.py:72
  83.2 0.7 fusion.19
  83.9 6.4 %all-to-all-done.2 = bf16[8,64,128]{2,1,0:T(8,128)(2,1)S(1)} async-done(((bf16[8,64,128]{2,1,0:T(8,128)(2,1)}), bf16[8,64,128]{2,1,0:T(8,128)(2,1)S(1)}, u32[]{:S(2)}, u32[]{:S(2)}) %all-to-all-start.2) | async-done | bytes 131104 | tf_op jit(solution)/shard_map/all_to_all | solution.py:72
  90.5 3.2 %convolution_convert_fusion = bf16[64,1024]{1,0:T(8,128)(2,1)S(1)} fusion(bf16[1024,1024]{1,0:T(8,128)(2,1)} %all-gather.4.cloned.1.call-done, f32[64,1024]{1,0:T(8,128)S(1)} %fusion.19, bf16[1,7,1024,128]{3,2,1,0:T(8,128)(2,1)} %param.11, bf16[64,1024]{1,0:T(8,128)(2,1)S(1)} %copy-done.2, bf16[7,64,128]{2,0,1:T(8,128)(2,1)S(1)} %convolution_convert_fusion.5), kind=kOutput, calls=%fused_computation.30 | convolution fusion | flops 251985920 | bytes 4571136 | tf_op jit(solution)/shard_map/dot_general | solution.py:52
  93.7 6.5 %all_gather.17 = bf16[256,1024]{1,0:T(8,128)(2,1)S(1)} all-gather(bf16[64,1024]{1,0:T(8,128)(2,1)S(1)} %convolution_convert_fusion), channel_id=1, replica_groups=mesh['tiles'=8,'rhs'=4] {'rhs'}, dimensions={0}, use_global_device_ids=true | all-gather | bytes 655360 | tf_op jit(solution)/shard_map/all_gather | solution.py:92
  100.4 0.7 scatter_custom_fusion.1
  101.2 30.9 %all-gather = f32[256,256]{1,0:T(8,128)S(1)} all-gather(f32[32,256]{1,0:T(8,128)S(1)} %scatter_custom_fusion.1), channel_id=2, replica_groups=mesh['tiles'=8,'rhs'=4] {'tiles'}, dimensions={0}, use_global_device_ids=true | all-gather | bytes 294912 | tf_op jit(solution)/shard_map/all_gather | solution.py:102
  132.1 0.6 constant_dynamic-slice_fusion
  (40 shorter events, 2.2 us)
Async XLA Ops:
  7.2 37.0 %copy-start = (bf16[1,7,1024,128]{3,2,1,0:T(8,128)(2,1)S(1)}, bf16[1,7,1024,128]{3,2,1,0:T(8,128)(2,1)}, u32[]{:S(2)}) copy-start(bf16[1,7,1024,128]{3,2,1,0:T(8,128)(2,1)} %param.12) | copy-start | bytes 5505028
  7.2 28.4 %all-gather.4.cloned.1.call-start = ((), (), s32[]{:S(2)}) async-start(), calls=%async_computation.4 | async-start | bytes 2621440 | tf_op jit(solution)/shard_map/all_gather | solution.py:49
  31.4 3.5 %copy-start.6 = (f32[8,32]{1,0:T(8,128)S(1)}, f32[8,32]{1,0:T(8,128)}, u32[]{:S(2)}) copy-start(f32[8,32]{1,0:T(8,128)} %param.16) | copy-start | bytes 3076
  31.4 3.6 %copy-start.4 = (f32[8,1024]{1,0:T(8,128)S(1)}, f32[8,1024]{1,0:T(8,128)}, u32[]{:S(2)}) copy-start(f32[8,1024]{1,0:T(8,128)} %param.15) | copy-start | bytes 98308
  31.4 3.6 %copy-start.7 = (s32[32]{0:T(128)S(1)}, s32[32]{0:T(128)}, u32[]{:S(2)}) copy-start(s32[32]{0:T(128)} %param.17) | copy-start | bytes 388
  31.4 3.8 %copy-start.8 = (s32[1,7]{1,0:T(1,128)S(1)}, s32[1,7]{1,0:T(1,128)}, u32[]{:S(2)}) copy-start(s32[1,7]{1,0:T(1,128)} %param.14) | copy-start | bytes 88
  31.4 4.2 %copy-start.2 = (bf16[64,1024]{1,0:T(8,128)(2,1)S(1)}, bf16[64,1024]{1,0:T(8,128)(2,1)}, u32[]{:S(2)}) copy-start(bf16[64,1024]{1,0:T(8,128)(2,1)} %param.9) | copy-start | bytes 393220
  35.6 2.2 %copy-start.1 = (bf16[1,7,1024,128]{3,2,1,0:T(8,128)(2,1)S(1)}, bf16[1,7,1024,128]{3,2,1,0:T(8,128)(2,1)}, u32[]{:S(2)}) copy-start(bf16[1,7,1024,128]{3,2,1,0:T(8,128)(2,1)} %param.11) | copy-start | bytes 5505028
  38.3 6.3 %copy-start.5 = (s32[1,7]{1,0:T(1,128)S(1)}, s32[1,7]{1,0:T(1,128)}, u32[]{:S(2)}) copy-start(s32[1,7]{1,0:T(1,128)} %param.13) | copy-start | bytes 88
  39.2 12.4 %all-to-all-start.1 = ((bf16[8,64,128]{2,1,0:T(8,128)(2,1)}), bf16[8,64,128]{2,1,0:T(8,128)(2,1)S(1)}, u32[]{:S(2)}, u32[]{:S(2)}) async-start(bf16[8,64,128]{2,1,0:T(8,128)(2,1)} %copy.50), calls=%async_computation.1 | async-start | bytes 262144 | tf_op jit(solution)/shard_map/all_to_all | solution.py:79
  51.6 10.7 %all-to-all-start = ((bf16[8,64,128]{2,1,0:T(8,128)(2,1)}), bf16[8,64,128]{2,1,0:T(8,128)(2,1)S(1)}, u32[]{:S(2)}, u32[]{:S(2)}) async-start(bf16[8,64,128]{2,1,0:T(8,128)(2,1)} %copy.45), calls=%async_computation | async-start | bytes 262144 | tf_op jit(solution)/shard_map/all_to_all | solution.py:72
  68.9 10.7 %all-to-all-start.3 = ((bf16[8,64,128]{2,1,0:T(8,128)(2,1)}), bf16[8,64,128]{2,1,0:T(8,128)(2,1)S(1)}, u32[]{:S(2)}, u32[]{:S(2)}) async-start(bf16[8,64,128]{2,1,0:T(8,128)(2,1)} %copy.60), calls=%async_computation.3 | async-start | bytes 262144 | tf_op jit(solution)/shard_map/all_to_all | solution.py:79
  79.6 10.7 %all-to-all-start.2 = ((bf16[8,64,128]{2,1,0:T(8,128)(2,1)}), bf16[8,64,128]{2,1,0:T(8,128)(2,1)S(1)}, u32[]{:S(2)}, u32[]{:S(2)}) async-start(bf16[8,64,128]{2,1,0:T(8,128)(2,1)} %copy.55), calls=%async_computation.2 | async-start | bytes 262144 | tf_op jit(solution)/shard_map/all_to_all | solution.py:72
  93.7 39.0 %copy-start.3 = (bf16[64,1024]{1,0:T(8,128)(2,1)}, bf16[64,1024]{1,0:T(8,128)(2,1)S(1)}, u32[]{:S(2)}) copy-start(bf16[64,1024]{1,0:T(8,128)(2,1)S(1)} %convolution_convert_fusion) | copy-start | bytes 393220
Sparse Core Ops, SparseCore 0:
  9.5 25.5 all-gather.3
